TPU v7x, 32 devices: a whole 2x2x4 slice. The times are simulated.
32 devices in a mesh: band: 2 (over x), tm: 16 (over z, y, core).
Axes of the slice: x: 2, y: 2, z: 4, core: 2. Of those that a mesh axis runs over, the one named last changes fastest.
Arguments:
- voltages: bfloat16 [65536, 2048], P(('band', 'tm')), parts along dimension 0, may hold values from -6 to 6
- panel_map: int32 [2048], replicated, may hold values from 0 to 2047, each once
- block_list: int32 [16, 2], replicated, may hold values from 0 to 15, as said below
Outputs:
- visibilities: float32 [32, 2, 256, 128, 128], P('band', None, 'tm'), parts along dimension 0
There are 2 independent parts, one for each index of `band`. A program takes and returns all parts, laid end to end along the dimension named above; an argument that names none is the same for every part. Nothing has to cross between parts.
Inputs may be any that keep to these rules, and one draw needn't show every extreme that they name: `block_list`: each row is a pair of panel numbers; the list names exactly 8 distinct panels, among them panel 0 and panel 16 - 1, every one of them in its first column.
All inputs are finite; a program needn't handle non-finite values.
Results may differ from a plain program's by a relative error of at most 0.0064.
Values may be sent and summed in bfloat16 or wider, within the bound.
No kernel may reach another device: no remote copies, remote signals or barrier semaphores. Data moves between devices by JAX's collectives and lax.ppermute only.
A program may use at most 128 MiB of HBM per device.

v0:
```python
import jax
import jax.numpy as jnp
from jax import lax
from jax.sharding import PartitionSpec as P

CHANNELS = 256
TAPS = 4
PANEL = 128


def from_behind(block, axis, distance):
    devices = range(lax.axis_size(axis))
    route = [(i - distance, i) for i in devices if i - distance in devices]
    return lax.ppermute(block, axis, route)


def filter_taps(taps, frame):
    length = taps * frame
    place = jnp.arange(length).astype(jnp.float32)
    middle = (length - 1) / 2.0
    window = 0.5 - 0.5 * jnp.cos(2.0 * jnp.pi * (place + 0.5) / length)
    shape_h = jnp.sinc((place - middle) / frame) * window
    shape_h = shape_h / jnp.sqrt(jnp.sum(shape_h * shape_h))
    return shape_h.reshape(taps, frame).astype(jnp.float32)


def dft_table(channels):
    frame = 2 * channels
    rows_k = jnp.arange(channels, dtype=jnp.int32)[:, None]
    cols_n = jnp.arange(frame, dtype=jnp.int32)[None, :]
    phase = (rows_k * cols_n % frame).astype(jnp.float32) * (2.0 * jnp.pi / frame)
    return jnp.concatenate([jnp.cos(phase), -jnp.sin(phase)], axis=0).astype(jnp.bfloat16)


def body(voltages, panel_map, block_list):
    frame = 2 * CHANNELS
    spec_dev = voltages.shape[0] // frame
    groups = lax.axis_size("tm")
    band_dev = CHANNELS // groups
    panel_rows = panel_map.reshape(-1, PANEL)
    columns = panel_rows[block_list]
    width = voltages.shape[1]
    frames = voltages.reshape(spec_dev, frame, width)
    earlier = from_behind(frames[spec_dev - (TAPS - 1) :], "tm", 1)
    padded = jnp.concatenate([earlier, frames], axis=0)
    coeff = filter_taps(TAPS, frame)
    filtered = jnp.zeros((spec_dev, frame, width), jnp.float32)
    for tap in range(TAPS):
        filtered = filtered + coeff[tap][None, :, None] * padded[tap : tap + spec_dev].astype(
            jnp.float32
        )
    filtered = filtered.astype(jnp.bfloat16)
    table = dft_table(CHANNELS)
    spectra = jnp.einsum("kn,sni->ski", table, filtered, preferred_element_type=jnp.float32)
    spectra = spectra.astype(jnp.bfloat16).reshape(spec_dev, 2, groups, band_dev, width)
    data = lax.all_to_all(spectra, "tm", split_axis=2, concat_axis=0, tiled=True)[:, :, 0]
    total = data.shape[0]
    first = data[:, :, :, columns[:, 0]]
    second = data[:, :, :, columns[:, 1]]
    flipped = jnp.stack([first[:, 1], -first[:, 0]], axis=1)
    real_part = jnp.einsum("sckbi,sckbj->bkij", first, second, preferred_element_type=jnp.float32)
    imag_part = jnp.einsum("sckbi,sckbj->bkij", flipped, second, preferred_element_type=jnp.float32)
    return jnp.stack([real_part, imag_part], axis=1) / total


def solution(mesh):
    in_specs = (P(("band", "tm"), None), P(), P())
    out_specs = P("band", None, "tm", None, None)
    return jax.shard_map(body, mesh=mesh, in_specs=in_specs, out_specs=out_specs, check_vma=False)
```

profile of v0, /device:TPU:13, one launch (start us, length us, event | category | flops | bytes accessed | tf_op | source)
XLA Modules:
  0.0 472.7 jit_solution(12410593673535821267)
XLA Ops:
  0.0 0.0 copy-start
  0.0 6.6 %slice.44 = bf16[1536,2048]{1,0:T(8,128)(2,1)} slice(bf16[2048,2048]{1,0:T(8,128)(2,1)} %param.3), slice={[512:2048], [0:2048]} | slice | bytes 12582912 | tf_op jit(solution)/shard_map/slice | solution.py:44
  6.6 3.7 collective-permute-start
  10.3 0.6 multiply_reduce_fusion
  11.6 0.1 broadcast_divide_fusion
  11.6 2.2 negate_convert_fusion
  13.8 64.7 %collective-permute-done = bf16[3,512,2048]{2,1,0:T(8,128)(2,1)} collective-permute-done((bf16[3,512,2048]{2,1,0:T(8,128)(2,1)}, bf16[3,512,2048]{2,1,0:T(8,128)(2,1)}, u32[]{:S(2)}, u32[]{:S(2)}) %collective-permute-start) | collective-permute-done | bytes 6291488 | tf_op jit(solution)/shard_map/ppermute | solution.py:14
  78.5 17.1 %fusion.6 = bf16[4,2048,512]{1,2,0:T(8,128)(2,1)} fusion(bf16[4,512,2048]{2,1,0:T(8,128)(2,1)} %bitcast.51, bf16[3,512,2048]{2,1,0:T(8,128)(2,1)} %collective-permute-done, f32[512]{0:T(512)S(1)} %get-tuple-element.10, f32[512]{0:T(512)S(1)} %get-tuple-element.11, f32[512]{0:T(512)S(1)} %get-tuple-element.12, f32[512]{0:T(512)S(1)} %get-tuple-element.9, ...), kind=kOutput, calls=%fused_computation.18 | convolution fusion | flops 4388290560 | bytes 23601152 | tf_op jit(solution)/shard_map/kn,sni->ski/dot_general | solution.py:54
  95.6 0.0 copy-start.2
  95.6 8.3 %copy.7 = bf16[4,2,16,16,2048]{4,3,1,0,2:T(8,128)(2,1)} copy(bf16[4,2,16,16,2048]{4,3,2,1,0:T(8,128)(2,1)} %bitcast.50) | data formatting | bytes 16777216 | tf_op jit(solution)/shard_map/reshape | solution.py:55
  103.9 7.2 %all-to-all-start = ((bf16[4,2,16,16,2048]{4,3,1,0,2:T(8,128)(2,1)}), bf16[4,2,16,16,2048]{4,3,1,0,2:T(8,128)(2,1)}, u32[]{:S(2)}, u32[]{:S(2)}) async-start(bf16[4,2,16,16,2048]{4,3,1,0,2:T(8,128)(2,1)} %copy.7), calls=%async_computation | async-start | bytes 16777216 | tf_op jit(solution)/shard_map/all_to_all | solution.py:56
  111.1 0.0 copy-done.2
  111.1 0.1 copy.8
  111.2 0.1 reshape.85
  111.3 0.0 copy-done
  111.3 0.6 gather_fusion
  112.0 181.5 %all-to-all-done = bf16[4,2,16,16,2048]{4,3,1,0,2:T(8,128)(2,1)} async-done(((bf16[4,2,16,16,2048]{4,3,1,0,2:T(8,128)(2,1)}), bf16[4,2,16,16,2048]{4,3,1,0,2:T(8,128)(2,1)}, u32[]{:S(2)}, u32[]{:S(2)}) %all-to-all-start) | async-done | bytes 8388640 | tf_op jit(solution)/shard_map/all_to_all | solution.py:56
  293.5 26.8 %copy.9 = bf16[64,2,16,2048]{0,2,3,1:T(8,128)(2,1)} copy(bf16[64,2,16,2048]{3,2,1,0:T(8,128)(2,1)} %bitcast.7) | data formatting | bytes 16777216 | tf_op jit(solution)/shard_map/squeeze | solution.py:56
  320.3 25.9 %gather_fusion.2 = bf16[2048,64,2,16]{1,3,2,0:T(8,128)(2,1)} fusion(bf16[64,2,16,2048]{0,2,3,1:T(8,128)(2,1)} %copy.9, s32[2048]{0:T(1024)S(1)} %fusion.26), kind=kCustom, calls=%fused_computation.2 | custom fusion | bytes 16785408 | tf_op jit(solution)/shard_map/gather | solution.py:59
  346.2 25.9 %gather_fusion.1 = bf16[2048,64,2,16]{1,3,2,0:T(8,128)(2,1)} fusion(bf16[64,2,16,2048]{0,2,3,1:T(8,128)(2,1)} %copy.9, s32[2048]{0:T(1024)S(1)} %fusion.24), kind=kCustom, calls=%fused_computation.1 | custom fusion | bytes 16785408 | tf_op jit(solution)/shard_map/gather | solution.py:58
  372.0 21.0 %copy.11 = bf16[16,128,64,2,16]{1,2,3,4,0:T(8,128)(2,1)} copy(bf16[16,128,64,2,16]{2,4,3,1,0:T(8,128)(2,1)} %bitcast.49) | data formatting | bytes 16777216 | tf_op jit(solution)/shard_map/gather | solution.py:58
  393.0 21.1 %copy.15 = bf16[64,2,16,16,128]{4,0,1,2,3:T(8,128)(2,1)} copy(bf16[64,2,16,16,128]{0,2,1,4,3:T(8,128)(2,1)} %bitcast.48) | data formatting | bytes 16777216 | tf_op jit(solution)/shard_map/gather | solution.py:59
  414.1 5.8 %fusion.35 = (bf16[64,1,16,16,128]{4,0,1,2,3:T(8,128)(2,1)}, bf16[64,1,16,16,128]{4,0,1,2,3:T(8,128)(2,1)}) fusion(bf16[64,2,16,16,128]{4,0,1,2,3:T(8,128)(2,1)} %bitcast.47), kind=kLoop, calls=%fused_computation.71 | loop fusion | flops 2097152 | bytes 16777216 | tf_op jit(solution)/shard_map/slice | solution.py:60
  419.9 14.4 %convolution_bitcast_fusion.1 = f32[16,1,16,128,128]{4,3,2,0,1:T(8,128)} fusion(bf16[64,2,16,16,128]{4,0,1,2,3:T(8,128)(2,1)} %copy.15, bf16[16,128,64,2,16]{1,2,3,4,0:T(8,128)(2,1)} %copy.11), kind=kOutput, calls=%fused_computation.10 | convolution fusion | flops 1073741824 | bytes 33554432 | tf_op jit(solution)/shard_map/sckbi,sckbj->bkij/dot_general | solution.py:61
  434.3 14.9 %convolution_bitcast_fusion = f32[16,1,16,128,128]{4,3,2,0,1:T(8,128)} fusion(bf16[64,2,16,16,128]{4,0,1,2,3:T(8,128)(2,1)} %copy.15, bf16[64,1,16,16,128]{4,0,1,2,3:T(8,128)(2,1)} %get-tuple-element.6, bf16[64,1,16,16,128]{4,0,1,2,3:T(8,128)(2,1)} %get-tuple-element.5), kind=kOutput, calls=%fused_computation.9 | convolution fusion | flops 1077936128 | bytes 33554432 | tf_op jit(solution)/shard_map/sckbi,sckbj->bkij/dot_general | solution.py:62
  449.2 12.2 %maximum_multiply_fusion = f32[16,2,16,128,128]{4,3,2,0,1:T(8,128)S(1)} fusion(f32[16,1,16,128,128]{4,3,2,0,1:T(8,128)} %convolution_bitcast_fusion, f32[16,1,16,128,128]{4,3,2,0,1:T(8,128)} %convolution_bitcast_fusion.1), kind=kLoop, calls=%fused_computation.3 | loop fusion | flops 16777216 | bytes 67108864 | tf_op jit(solution)/shard_map/div | solution.py:63
  461.4 0.0 copy-start.1
  461.4 11.3 %copy.17 = f32[16,2,16,128,128]{4,3,2,1,0:T(8,128)} copy(f32[16,2,16,128,128]{4,3,2,0,1:T(8,128)S(1)} %maximum_multiply_fusion) | data formatting | bytes 67108864 | tf_op jit(solution)/shard_map/div | solution.py:63
  472.7 0.0 copy-done.1
  (6 shorter events, 0.0 us)
Async XLA Ops:
  0.0 111.3 %copy-start = (s32[2048]{0:T(1024)S(1)}, s32[2048]{0:T(1024)}, u32[]{:S(2)}) copy-start(s32[2048]{0:T(1024)} %param.4) | copy-start | bytes 24580
  6.6 71.9 %collective-permute-start = (bf16[3,512,2048]{2,1,0:T(8,128)(2,1)}, bf16[3,512,2048]{2,1,0:T(8,128)(2,1)}, u32[]{:S(2)}, u32[]{:S(2)}) collective-permute-start(bf16[3,512,2048]{2,1,0:T(8,128)(2,1)} %bitcast), channel_id=1, source_target_pairs={{0,1},{1,2},{2,3},{3,4},{4,5},{5,6},{6,7},{7,8},{8,9},{9,10},{10,1... | collective-permute-start | bytes 18874376 | tf_op jit(solution)/shard_map/ppermute | solution.py:14
  95.6 15.5 %copy-start.2 = (s32[16,2]{0,1:T(2,128)S(1)}, s32[16,2]{0,1:T(2,128)}, u32[]{:S(2)}) copy-start(s32[16,2]{0,1:T(2,128)} %param.5) | copy-start | bytes 388
  103.9 189.6 %all-to-all-start = ((bf16[4,2,16,16,2048]{4,3,1,0,2:T(8,128)(2,1)}), bf16[4,2,16,16,2048]{4,3,1,0,2:T(8,128)(2,1)}, u32[]{:S(2)}, u32[]{:S(2)}) async-start(bf16[4,2,16,16,2048]{4,3,1,0,2:T(8,128)(2,1)} %copy.7), calls=%async_computation | async-start | bytes 16777216 | tf_op jit(solution)/shard_map/all_to_all | solution.py:56
  461.4 11.3 %copy-start.1 = (s32[2048]{0:T(1024)S(1)}, s32[2048]{0:T(1024)}, u32[]{:S(2)}) copy-start(s32[2048]{0:T(1024)} %param.4) | copy-start | bytes 24580
where the time goes:
time: 474 us; the launch traced here: 473 us
  waiting for transfers between devices  246 us (52%)
  local copies, waits for them, and re-layouts  148 us (31%)
  matrix products  46.3 us (10%)
  other arithmetic  20.9 us (4%)
  starting transfers between devices  10.9 us (2%)
    all_to_all x1, waiting for transfers between devices, body(): lax.all_to_all(spectra, 'tm', split_axis=2, concat_axis=0, tiled=True)  182 us
    ppermute x1, waiting for transfers between devices, from_behind(): return lax.ppermute(block, axis, route)  64.7 us
    gather x2, local copies, waits for them, and re-layouts, body(): second = data[:, :, :, columns[:, 1]]  46.9 us
    gather x2, local copies, waits for them, and re-layouts, body(): first = data[:, :, :, columns[:, 0]]  46.9 us
    squeeze x1, local copies, waits for them, and re-layouts, body(): lax.all_to_all(spectra, 'tm', split_axis=2, concat_axis=0, tiled=True)  26.8 us
    dot_general x1, matrix products, body(): jnp.einsum('kn,sni->ski', table, filtered, preferred_element_type=jnp.flo...  17.1 us
    dot_general x1, matrix products, body(): jnp.einsum('sckbi,sckbj->bkij', flipped, second, preferred_element_type=j...  14.9 us
    dot_general x1, matrix products, body(): jnp.einsum('sckbi,sckbj->bkij', first, second, preferred_element_type=jnp...  14.4 us
  transfers between devices with their start and end apart: 2, of which 2 were waited for; matrix products, arithmetic and copies ran while one was open for 1% of the time, Pallas kernels for 0%

commit v1 on v0

--- a/solution.py
+++ b/solution.py
@@ -53,7 +53,10 @@
     table = dft_table(CHANNELS)
     spectra = jnp.einsum("kn,sni->ski", table, filtered, preferred_element_type=jnp.float32)
     spectra = spectra.astype(jnp.bfloat16).reshape(spec_dev, 2, groups, band_dev, width)
-    data = lax.all_to_all(spectra, "tm", split_axis=2, concat_axis=0, tiled=True)[:, :, 0]
+    data = jnp.concatenate(
+        lax.all_to_all(jnp.stack(jnp.split(spectra, lax.axis_size("tm"), axis=2)), "tm", 0, 0),
+        axis=0,
+    )[:, :, 0]
     total = data.shape[0]
     first = data[:, :, :, columns[:, 0]]
     second = data[:, :, :, columns[:, 1]]

time: 474 us -> 477 us (level)
  local copies, waits for them, and re-layouts: 148 us -> 153 us
    another operation x0 -> x2, local copies, waits for them, and re-layouts: none -> 27.6 us  [the longest x1 26.8 us: body(): jnp.concatenate(lax.all_to_all(jnp.stack(jnp.split(spectra, lax.axis_size...]
    squeeze x1 -> x0, local copies, waits for them, and re-layouts: 26.8 us -> none  [body(): lax.all_to_all(spectra, 'tm', split_axis=2, concat_axis=0, tiled=True)]
    unnamed x6 -> x21, local copies, waits for them, and re-layouts: 0.01 us -> 12.5 us
    reshape x1 -> x0, local copies, waits for them, and re-layouts: 8.28 us -> none  [body(): spectra.astype(jnp.bfloat16).reshape(spec_dev, 2, groups, band_dev, width)]
where the time goes in v1:
time: 477 us; the launch traced here: 476 us
  waiting for transfers between devices  246 us (52%)
  local copies, waits for them, and re-layouts  153 us (32%)
  matrix products  44.2 us (9%)
  other arithmetic  20.9 us (4%)
  starting transfers between devices  11.1 us (2%)
    all_to_all x1, waiting for transfers between devices, body(): lax.all_to_all(jnp.stack(jnp.split(spectra, lax.axis_size('tm'), axis=2))...  182 us
    ppermute x1, waiting for transfers between devices, from_behind(): return lax.ppermute(block, axis, route)  64.6 us
    gather x2, local copies, waits for them, and re-layouts, body(): second = data[:, :, :, columns[:, 1]]  46.9 us
    gather x2, local copies, waits for them, and re-layouts, body(): first = data[:, :, :, columns[:, 0]]  46.9 us
    another operation x1, local copies, waits for them, and re-layouts, body(): jnp.concatenate(lax.all_to_all(jnp.stack(jnp.split(spectra, lax.axis_size...  26.8 us
    dot_general x1, matrix products, body(): jnp.einsum('kn,sni->ski', table, filtered, preferred_element_type=jnp.flo...  14.9 us
    dot_general x1, matrix products, body(): jnp.einsum('sckbi,sckbj->bkij', flipped, second, preferred_element_type=j...  14.9 us
    dot_general x1, matrix products, body(): jnp.einsum('sckbi,sckbj->bkij', first, second, preferred_element_type=jnp...  14.4 us
  transfers between devices with their start and end apart: 2, of which 2 were waited for; matrix products, arithmetic and copies ran while one was open for 1% of the time, Pallas kernels for 0%

profile of v1, /device:TPU:13, one launch (start us, length us, event | category | flops | bytes accessed | tf_op | source)
XLA Modules:
  0.0 475.7 jit_solution(16743682987663693089)
XLA Ops:
  0.0 0.0 copy-start
  0.0 6.6 %slice.44 = bf16[1536,2048]{1,0:T(8,128)(2,1)} slice(bf16[2048,2048]{1,0:T(8,128)(2,1)} %param.3), slice={[512:2048], [0:2048]} | slice | bytes 12582912 | tf_op jit(solution)/shard_map/slice | solution.py:44
  6.6 3.7 collective-permute-start
  10.3 0.7 multiply_reduce_fusion
  11.7 0.1 broadcast_divide_fusion
  11.7 2.2 negate_convert_fusion
  13.9 64.6 %collective-permute-done = bf16[3,512,2048]{2,1,0:T(8,128)(2,1)} collective-permute-done((bf16[3,512,2048]{2,1,0:T(8,128)(2,1)}, bf16[3,512,2048]{2,1,0:T(8,128)(2,1)}, u32[]{:S(2)}, u32[]{:S(2)}) %collective-permute-start) | collective-permute-done | bytes 6291488 | tf_op jit(solution)/shard_map/ppermute | solution.py:14
  78.5 14.9 %fusion.6 = bf16[4,2048,512]{1,2,0:T(8,128)(2,1)S(1)} fusion(bf16[4,512,2048]{2,1,0:T(8,128)(2,1)} %bitcast.158, bf16[3,512,2048]{2,1,0:T(8,128)(2,1)} %collective-permute-done, f32[512]{0:T(512)S(1)} %get-tuple-element.10, f32[512]{0:T(512)S(1)} %get-tuple-element.11, f32[512]{0:T(512)S(1)} %get-tuple-element.12, f32[512]{0:T(512)S(1)} %get-tuple-element.9, ...), kind=kOutput, calls=%fused_computation.18 | convolution fusion | flops 4388290560 | bytes 23601152 | tf_op jit(solution)/shard_map/kn,sni->ski/dot_general | solution.py:54
  93.5 0.8 fusion.25
  94.3 0.8 fusion.24
  95.2 0.8 fusion.23
  96.0 0.8 fusion.22
  96.8 0.8 fusion.21
  97.6 0.8 fusion.20
  98.5 0.8 fusion.19
  99.3 0.8 fusion.18
  100.1 0.8 fusion.17
  101.0 0.8 fusion.16
  101.8 0.8 fusion.15
  102.6 0.8 fusion.14
  103.5 0.8 fusion.13
  104.3 0.8 fusion.12
  105.1 0.8 fusion.11
  106.0 0.8 fusion.10
  106.8 0.0 copy-start.2
  106.8 7.4 %all-to-all-start = ((bf16[16,4,2,1,16,2048]{5,4,2,1,3,0:T(8,128)(2,1)}), bf16[16,4,2,1,16,2048]{5,4,2,1,3,0:T(8,128)(2,1)}, u32[]{:S(2)}, u32[]{:S(2)}) async-start(bf16[16,4,2,1,16,2048]{5,4,2,1,3,0:T(8,128)(2,1)} %fusion.10), calls=%async_computation | async-start | bytes 16777216 | tf_op jit(solution)/shard_map/all_to_all | solution.py:57
  114.2 0.0 copy-done.2
  114.2 0.1 copy.88
  114.3 0.1 reshape.84
  114.4 0.0 copy-done
  114.4 0.6 gather_fusion
  115.0 181.5 %all-to-all-done = bf16[16,4,2,1,16,2048]{5,4,2,1,3,0:T(8,128)(2,1)} async-done(((bf16[16,4,2,1,16,2048]{5,4,2,1,3,0:T(8,128)(2,1)}), bf16[16,4,2,1,16,2048]{5,4,2,1,3,0:T(8,128)(2,1)}, u32[]{:S(2)}, u32[]{:S(2)}) %all-to-all-start) | async-done | bytes 8388640 | tf_op jit(solution)/shard_map/all_to_all | solution.py:57
  296.5 26.8 %copy.89 = bf16[64,2,16,2048]{0,2,3,1:T(8,128)(2,1)} copy(bf16[64,2,16,2048]{3,2,1,0:T(8,128)(2,1)} %bitcast.22) | data formatting | bytes 16777216 | tf_op jit(solution)/shard_map/squeeze;reshape | solution.py:56
  323.3 25.9 %gather_fusion.2 = bf16[2048,64,2,16]{1,3,2,0:T(8,128)(2,1)} fusion(bf16[64,2,16,2048]{0,2,3,1:T(8,128)(2,1)} %copy.89, s32[2048]{0:T(1024)S(1)} %get-tuple-element.16), kind=kCustom, calls=%fused_computation.2 | custom fusion | bytes 16785408 | tf_op jit(solution)/shard_map/gather | solution.py:62
  349.2 25.9 %gather_fusion.1 = bf16[2048,64,2,16]{1,3,2,0:T(8,128)(2,1)} fusion(bf16[64,2,16,2048]{0,2,3,1:T(8,128)(2,1)} %copy.89, s32[2048]{0:T(1024)S(1)} %get-tuple-element.15), kind=kCustom, calls=%fused_computation.1 | custom fusion | bytes 16785408 | tf_op jit(solution)/shard_map/gather | solution.py:61
  375.0 21.0 %copy.91 = bf16[16,128,64,2,16]{1,2,3,4,0:T(8,128)(2,1)} copy(bf16[16,128,64,2,16]{2,4,3,1,0:T(8,128)(2,1)} %bitcast.141) | data formatting | bytes 16777216 | tf_op jit(solution)/shard_map/gather | solution.py:61
  396.0 21.1 %copy.95 = bf16[64,2,16,16,128]{4,0,1,2,3:T(8,128)(2,1)} copy(bf16[64,2,16,16,128]{0,2,1,4,3:T(8,128)(2,1)} %bitcast.140) | data formatting | bytes 16777216 | tf_op jit(solution)/shard_map/gather | solution.py:62
  417.1 5.8 %fusion.51 = (bf16[64,1,16,16,128]{4,0,1,2,3:T(8,128)(2,1)}, bf16[64,1,16,16,128]{4,0,1,2,3:T(8,128)(2,1)}) fusion(bf16[64,2,16,16,128]{4,0,1,2,3:T(8,128)(2,1)} %bitcast.139), kind=kLoop, calls=%fused_computation.103 | loop fusion | flops 2097152 | bytes 16777216 | tf_op jit(solution)/shard_map/slice | solution.py:63
  422.9 14.4 %convolution_bitcast_fusion.1 = f32[16,1,16,128,128]{4,3,2,0,1:T(8,128)} fusion(bf16[64,2,16,16,128]{4,0,1,2,3:T(8,128)(2,1)} %copy.95, bf16[16,128,64,2,16]{1,2,3,4,0:T(8,128)(2,1)} %copy.91), kind=kOutput, calls=%fused_computation.10 | convolution fusion | flops 1073741824 | bytes 33554432 | tf_op jit(solution)/shard_map/sckbi,sckbj->bkij/dot_general | solution.py:64
  437.3 14.9 %convolution_bitcast_fusion = f32[16,1,16,128,128]{4,3,2,0,1:T(8,128)} fusion(bf16[64,2,16,16,128]{4,0,1,2,3:T(8,128)(2,1)} %copy.95, bf16[64,1,16,16,128]{4,0,1,2,3:T(8,128)(2,1)} %get-tuple-element.6, bf16[64,1,16,16,128]{4,0,1,2,3:T(8,128)(2,1)} %get-tuple-element.5), kind=kOutput, calls=%fused_computation.9 | convolution fusion | flops 1077936128 | bytes 33554432 | tf_op jit(solution)/shard_map/sckbi,sckbj->bkij/dot_general | solution.py:65
  452.2 12.2 %maximum_multiply_fusion = f32[16,2,16,128,128]{4,3,2,0,1:T(8,128)S(1)} fusion(f32[16,1,16,128,128]{4,3,2,0,1:T(8,128)} %convolution_bitcast_fusion, f32[16,1,16,128,128]{4,3,2,0,1:T(8,128)} %convolution_bitcast_fusion.1), kind=kLoop, calls=%fused_computation.3 | loop fusion | flops 16777216 | bytes 67108864 | tf_op jit(solution)/shard_map/div | solution.py:66
  464.4 0.0 copy-start.1
  464.4 11.3 %copy.97 = f32[16,2,16,128,128]{4,3,2,1,0:T(8,128)} copy(f32[16,2,16,128,128]{4,3,2,0,1:T(8,128)S(1)} %maximum_multiply_fusion) | data formatting | bytes 67108864 | tf_op jit(solution)/shard_map/div | solution.py:66
  475.7 0.0 copy-done.1
  (5 shorter events, 0.0 us)
Async XLA Ops:
  0.0 114.4 %copy-start = (s32[2048]{0:T(1024)S(1)}, s32[2048]{0:T(1024)}, u32[]{:S(2)}) copy-start(s32[2048]{0:T(1024)} %param.4) | copy-start | bytes 24580
  6.6 71.9 %collective-permute-start = (bf16[3,512,2048]{2,1,0:T(8,128)(2,1)}, bf16[3,512,2048]{2,1,0:T(8,128)(2,1)}, u32[]{:S(2)}, u32[]{:S(2)}) collective-permute-start(bf16[3,512,2048]{2,1,0:T(8,128)(2,1)} %bitcast), channel_id=1, source_target_pairs={{0,1},{1,2},{2,3},{3,4},{4,5},{5,6},{6,7},{7,8},{8,9},{9,10},{10,1... | collective-permute-start | bytes 18874376 | tf_op jit(solution)/shard_map/ppermute | solution.py:14
  106.8 7.4 %copy-start.2 = (s32[16,2]{0,1:T(2,128)S(1)}, s32[16,2]{0,1:T(2,128)}, u32[]{:S(2)}) copy-start(s32[16,2]{0,1:T(2,128)} %param.5) | copy-start | bytes 388
  106.8 189.7 %all-to-all-start = ((bf16[16,4,2,1,16,2048]{5,4,2,1,3,0:T(8,128)(2,1)}), bf16[16,4,2,1,16,2048]{5,4,2,1,3,0:T(8,128)(2,1)}, u32[]{:S(2)}, u32[]{:S(2)}) async-start(bf16[16,4,2,1,16,2048]{5,4,2,1,3,0:T(8,128)(2,1)} %fusion.10), calls=%async_computation | async-start | bytes 16777216 | tf_op jit(solution)/shard_map/all_to_all | solution.py:57
  464.4 11.3 %copy-start.1 = (s32[2048]{0:T(1024)S(1)}, s32[2048]{0:T(1024)}, u32[]{:S(2)}) copy-start(s32[2048]{0:T(1024)} %param.4) | copy-start | bytes 24580
